TPU v7x, 32 devices: a whole 2x2x4 slice. The times are simulated.
32 devices in a mesh: row: 8 (over z, y), col: 4 (over x, core).
Axes of the slice: x: 2, y: 2, z: 4, core: 2. Of those that a mesh axis runs over, the one named last changes fastest.
Arguments:
- load_currents: float32 [32, 1024, 512], P(None, 'row', 'col'), may hold values from -36 to 36
- labels: int32 [1024, 512], P('row', 'col'), may hold values from 0 to 255, as said below
- bump_height: float32 [1024, 512], P('row', 'col'), may hold values from 0.5 to 2
- horizontal_class: int32 [1024, 512], P('row', 'col'), may hold values from 0 to 7
- vertical_class: int32 [1024, 512], P('row', 'col'), may hold values from 0 to 7
- pad_class: int32 [1024, 512], P('row', 'col'), may hold values from 0 to 7
- edge_table: float32 [8], replicated, may hold values from 0.5 to 4
- pad_table: float32 [8], replicated, may hold values from 0.02 to 0.5
Outputs:
- solution: float32 [32, 1024, 512], P(None, 'row', 'col')
- residual: float32 [32, 1024, 512], P(None, 'row', 'col')
Inputs may be any that keep to these rules, and one draw needn't show every extreme that they name: `labels`: every number from 0 to 255 is the label of some nodes; the label of node (i, j) is 16 * floor(16 * i2 / 1024) + floor(16 * j2 / 512) for some node (i2, j2) of the grid with |i2 - i| <= 16 and |j2 - j| <= 8.
All inputs are finite; a program needn't handle non-finite values.
Results may differ from a plain program's by a relative error of at most 0.0003.
Values sent between devices are 32-bit elements; how exact they have to be, the bound alone decides.
A program may use at most 128 MiB of HBM per device.

v0:
```python
import jax
import jax.numpy as jnp
from jax import lax
from jax.sharding import PartitionSpec as P

REG = 16
ITERS = 2
precise = lax.Precision.HIGHEST


def from_behind(value, axis, steps):
    count = lax.axis_size(axis)
    initial, last = (max(0, -steps), min(count, count - steps))
    return lax.ppermute(value, axis, [(source, source + steps) for source in range(initial, last)])


def extended(value, sides, width):
    for axis, dim in sides:
        size, length = (lax.axis_size(axis), value.shape[dim])
        up = [(i, (i + 1) % size) for i in range(size - 1)]
        down = [(j, i) for i, j in up]
        last = lax.slice_in_dim(value, length - width, length, axis=dim)
        initial = lax.slice_in_dim(value, 0, width, axis=dim)
        before = lax.ppermute(last, axis, up)
        after = lax.ppermute(initial, axis, down)
        value = jnp.concatenate([before, value, after], axis=dim)
    return value


def lookup(entries, classes):
    levels = lax.broadcasted_iota(jnp.int32, (entries.shape[0],) + classes.shape, 0)
    return jnp.sum(jnp.where(classes[None] == levels, entries[:, None, None], 0.0), axis=0)


def stencil(padded, coeffs):
    diagonal, right_link, left_link, down_link, upper_link = coeffs
    centre = padded[:, 1:-1, 1:-1]
    return (
        diagonal * centre
        - right_link * padded[:, 1:-1, 2:]
        - left_link * padded[:, 1:-1, :-2]
        - down_link * padded[:, 2:, 1:-1]
        - upper_link * padded[:, :-2, 1:-1]
    )


def invert(matrix):
    factor = jnp.linalg.cholesky(matrix)
    identity = jnp.eye(matrix.shape[0], dtype=matrix.dtype)
    lower_solved = lax.linalg.triangular_solve(factor, identity, left_side=True, lower=True)
    return lax.linalg.triangular_solve(
        factor, lower_solved, left_side=True, lower=True, transpose_a=True
    )


def body(
    load_currents,
    labels,
    bump_height,
    horizontal_class,
    vertical_class,
    pad_class,
    edge_table,
    pad_table,
):
    tile_rows, tile_cols = labels.shape
    regions = REG * REG
    load_count = load_currents.shape[0]
    tile_cells = tile_rows * tile_cols
    grid_rows = lax.axis_size("row") * tile_rows
    grid_cols = lax.axis_size("col") * tile_cols
    row_ids = lax.axis_index("row") * tile_rows + lax.broadcasted_iota(jnp.int32, labels.shape, 0)
    col_ids = lax.axis_index("col") * tile_cols + lax.broadcasted_iota(jnp.int32, labels.shape, 1)
    right_link = jnp.where(col_ids == grid_cols - 1, 0.0, lookup(edge_table, horizontal_class))
    down_link = jnp.where(row_ids == grid_rows - 1, 0.0, lookup(edge_table, vertical_class))
    left_edge = from_behind(right_link[:, -1:], "col", 1)
    left_link = jnp.concatenate([left_edge, right_link[:, :-1]], axis=1)
    upper_edge = from_behind(down_link[-1:, :], "row", 1)
    upper_link = jnp.concatenate([upper_edge, down_link[:-1, :]], axis=0)
    diagonal = lookup(pad_table, pad_class) + right_link + left_link + down_link + upper_link
    coeffs = (diagonal, right_link, left_link, down_link, upper_link)
    levels = lax.broadcasted_iota(jnp.int32, (regions,) + labels.shape, 0)
    deflation = jnp.where(labels[None] == levels, bump_height[None], 0.0)
    deflation_image = stencil(extended(deflation, (("row", 1), ("col", 2)), 1), coeffs)
    basis_flat = deflation.reshape(regions, tile_cells)
    image_flat = deflation_image.reshape(regions, tile_cells)
    contract = (((1,), (1,)), ((), ()))
    partial_matrix = lax.dot_general(basis_flat, image_flat, contract, precision=precise)
    inverse = invert(lax.psum(partial_matrix, ("row", "col")))

    def project(field):
        return lax.dot_general(
            field.reshape(load_count, tile_cells), basis_flat, contract, precision=precise
        )

    def expand(coarse):
        return jnp.dot(coarse, basis_flat, precision=precise).reshape(
            load_count, tile_rows, tile_cols
        )

    def correction_image(coarse):
        return jnp.dot(coarse, image_flat, precision=precise).reshape(
            load_count, tile_rows, tile_cols
        )

    def refresh(residual):
        scaled = residual / diagonal
        local_norm = jnp.sum(residual * scaled, axis=(1, 2))
        field_image = stencil(extended(scaled, (("row", 1), ("col", 2)), 1), coeffs)
        weighted_norm = lax.psum(local_norm, ("row", "col"))
        projected = lax.psum(project(field_image), ("row", "col"))
        coarse = jnp.dot(projected, inverse, precision=precise)
        return (scaled, weighted_norm, field_image, coarse)

    load_sums = lax.psum(project(load_currents), ("row", "col"))
    coarse = jnp.dot(load_sums, inverse, precision=precise)
    solution = expand(coarse)
    residual = load_currents - correction_image(coarse)
    scaled, weighted_norm, field_image, coarse = refresh(residual)
    spread = expand(coarse)
    direction = scaled - spread
    direction_image = field_image - correction_image(coarse)
    for iteration in range(ITERS):
        local_curve = jnp.sum(direction * direction_image, axis=(1, 2))
        curvature = lax.psum(local_curve, ("row", "col"))
        step_size = (weighted_norm / curvature)[:, None, None]
        solution = solution + step_size * direction
        residual = residual - step_size * direction_image
        if iteration + 1 < ITERS:
            scaled, new_norm, field_image, coarse = refresh(residual)
            spread = expand(coarse)
            beta_ratio = (new_norm / weighted_norm)[:, None, None]
            direction = scaled - spread + beta_ratio * direction
            direction_image = field_image - correction_image(coarse) + beta_ratio * direction_image
            weighted_norm = new_norm
    return (solution, residual)


def solution(mesh):
    return jax.shard_map(
        body,
        mesh=mesh,
        in_specs=(
            P(None, "row", "col"),
            P("row", "col"),
            P("row", "col"),
            P("row", "col"),
            P("row", "col"),
            P("row", "col"),
            P(),
            P(),
        ),
        out_specs=(P(None, "row", "col"), P(None, "row", "col")),
        check_vma=False,
    )
```

profile of v0, /device:TPU:0, one launch (start us, length us, event | category | flops | bytes accessed | tf_op | source)
XLA Modules:
  0.0 716.1 jit_solution(5788398756781292680)
XLA Ops:
  7.2 1.1 select_reduce_fusion.1
  8.4 2.4 collective-permute-start
  11.0 4.4 collective-permute-start.1
  15.3 5.4 fusion.28
  20.8 3.4 collective-permute-start.2
  24.3 1.4 collective-permute-start.3
  25.7 18.0 %fusion.84 = f32[32,256]{1,0:T(8,128)S(1)} fusion(f32[32,128,128]{2,1,0:T(8,128)S(1)} %copy-done.11, f32[128,128]{1,0:T(8,128)S(1)} %copy-done.12, s32[128,128]{1,0:T(8,128)S(1)} %copy-done.13), kind=kOutput, calls=%fused_computation.114 | convolution fusion | flops 1619001344 | bytes 2260992 | tf_op jit(solution)/shard_map/dot_general | solution.py:92
  44.1 1.3 collective-permute-start.4
  45.4 3.8 collective-permute-start.5
  49.3 0.8 collective-permute-done.5
  50.1 31.3 %fusion.17 = f32[256,128,128]{0,2,1:T(8,128)S(1)} fusion(f32[256,128,128]{0,2,1:T(8,128)} %copy-done.1, f32[256,1,128]{0,2,1:T(8,128)S(1)} %collective-permute-done.2, f32[256,1,128]{0,2,1:T(8,128)S(1)} %collective-permute-done.3, f32[256,130,1]{0,2,1:T(1,128)S(1)} %collective-permute-done.5, f32[256,130,1]{0,2,1:T(1,128)S(1)} %collective-permute-done.4, ...), kind=kLoop, calls=%fused_computation.20 | loop fusion | flops 79691776 | bytes 34541568 | tf_op jit(solution)/shard_map/sub | solution.py:39
  81.5 5.7 copy-done
  87.2 38.4 %fusion.81 = f32[256,256]{0,1:T(8,128)} fusion(f32[256,128,128]{0,2,1:T(8,128)S(1)} %fusion.17, f32[128,128]{1,0:T(8,128)S(1)} %copy-done.12, s32[128,128]{1,0:T(8,128)S(1)} %copy-done.13), kind=kOutput, calls=%fused_computation.110 | convolution fusion | flops 12893290496 | bytes 17170432 | tf_op jit(solution)/shard_map/dot_general | solution.py:88
  125.7 45.2 %psum.56 = f32[32,256]{1,0:T(8,128)S(1)} all-reduce(f32[32,256]{1,0:T(8,128)S(1)} %fusion.84), channel_id=1, replica_groups=mesh['row'=8,'col'=4] {'row','col'}, use_global_device_ids=true, to_apply=%region_0.1 | all-reduce | flops 8192 | bytes 65536 | tf_op jit(solution)/shard_map/psum | solution.py:115
  170.9 87.1 %all-reduce.5.cloned.1.call-done = f32[256,256]{0,1:T(8,128)} async-done(((f32[256,256]{0,1:T(8,128)}), f32[256,256]{0,1:T(8,128)}) %all-reduce.5.cloned.1.call-update) | async-done | bytes 262160 | tf_op jit(solution)/shard_map/psum | solution.py:89
  258.0 1.1 copy.46
  259.1 1.0 fusion.95
  260.1 11.7 %cholesky.53 = f32[128,128]{1,0:T(8,128)S(1)} custom-call(f32[128,128]{1,0:T(8,128)S(1)} %cholesky.121), custom_call_target="Cholesky" | custom-call | tf_op jit(solution)/shard_map/jit(cholesky)/cholesky | solution.py:48
  271.9 9.8 %custom-call.16 = f32[1,128,128]{1,2,0:T(8,128)S(1)} custom-call(f32[1,128,128]{2,1,0:T(8,128)S(1)} %get-tuple-element.56), custom_call_target="InvertDiagBlocksLowerTriangular" | custom-call | tf_op jit(solution)/shard_map/jit(cholesky)/cholesky | solution.py:48
  282.2 11.7 %cholesky.108 = f32[128,128]{1,0:T(8,128)S(1)} custom-call(f32[128,128]{1,0:T(8,128)S(1)} %convolution_subtract_fusion.2), custom_call_target="Cholesky" | custom-call | tf_op jit(solution)/shard_map/jit(cholesky)/cholesky | solution.py:48
  296.1 4.1 while.1
  296.7 1.4 bitcast_dynamic-update-slice_fusion.2
  298.7 1.4 bitcast_dynamic-update-slice_fusion.2
  300.2 20.1 %custom-call.17 = f32[2,128,128]{1,2,0:T(8,128)S(1)} custom-call(f32[2,128,128]{2,1,0:T(8,128)S(1)} %get-tuple-element.9), custom_call_target="InvertDiagBlocksLowerTriangular" | custom-call | tf_op jit(solution)/shard_map/triangular_solve | solution.py:51
  322.2 18.5 %multiply_reduce_fusion.3 = (f32[32]{0:T(128)S(1)}, f32[32,128,128]{2,0,1:T(8,128)S(1)}, f32[32,128,128]{2,0,1:T(8,128)}) fusion(f32[128,128]{1,0:T(8,128)S(1)} %get-tuple-element.34, f32[32,256,1]{1,0,2:T(8,128)S(1)} %convolution_bitcast_fusion.2, f32[256,128,128]{0,2,1:T(8,128)} %copy-done, f32[32,128,128]{2,1,0:T(8,128)} %param.8), kind=kOutput, calls=%fused_computation.105 | convolution fusion | flops 1612709888 | bytes 23167104 | tf_op jit(solution)/shard_map/dot_general | solution.py:102
  340.7 3.4 collective-permute-start.6
  344.1 1.3 collective-permute-start.7
  345.5 4.2 collective-permute-done.7
  349.9 2.7 fusion.119
  352.7 3.2 copy.48
  355.9 1.3 collective-permute-start.8
  357.2 3.2 copy.50
  360.4 3.2 collective-permute-start.9
  363.6 3.6 copy.49
  367.1 3.6 copy.51
  370.7 4.6 fusion.59
  375.4 1.3 copy-done.10
  376.7 16.4 %fusion.89 = f32[32,256]{1,0:T(8,128)S(1)} fusion(f32[32,128,128]{2,0,1:T(8,128)S(1)} %fusion.59, f32[128,128]{1,0:T(8,128)S(1)} %copy-done.12, s32[128,128]{1,0:T(8,128)S(1)} %copy-done.13), kind=kOutput, calls=%fused_computation.115 | convolution fusion | flops 1619001344 | bytes 2260992 | tf_op jit(solution)/shard_map/dot_general | solution.py:92
  393.1 40.3 %psum.59 = f32[32,256]{1,0:T(8,128)S(1)} all-reduce(f32[32,256]{1,0:T(8,128)S(1)} %fusion.89), channel_id=1, replica_groups=mesh['row'=8,'col'=4] {'row','col'}, use_global_device_ids=true, to_apply=%region_11.12 | all-reduce | flops 8192 | bytes 65536 | tf_op jit(solution)/shard_map/psum | solution.py:111
  433.7 17.8 %fusion.76 = f32[32,128,128]{2,0,1:T(8,128)S(1)} fusion(f32[32,128,128]{2,0,1:T(8,128)} %copy-done.10, f32[32,256,1]{1,0,2:T(8,128)S(1)} %convolution_bitcast_fusion.1, f32[256,128,128]{0,2,1:T(8,128)} %copy-done), kind=kOutput, calls=%fused_computation.109 | convolution fusion | flops 1611137024 | bytes 21004288 | tf_op jit(solution)/shard_map/dot_general | solution.py:102
  451.6 20.1 %multiply_reduce_fusion.2 = (f32[32]{0:T(128)S(1)}, f32[32,128,128]{2,0,1:T(8,128)}) fusion(f32[32,128,128]{2,0,1:T(8,128)S(1)} %fusion.76, f32[32,256,1]{1,0,2:T(8,128)S(1)} %convolution_bitcast_fusion.1, f32[128,128]{1,0:T(8,128)S(1)} %copy-done.12, s32[128,128]{1,0:T(8,128)S(1)} %copy-done.13, f32[32,128,128]{2,0,1:T(8,128)S(1)} %copy-done.8, ...), kind=kOutput, calls=%fused_computation.104 | convolution fusion | flops 1621098496 | bytes 6520960 | tf_op jit(solution)/shard_map/dot_general | solution.py:97
  471.6 39.8 %all-reduce.2 = (f32[32]{0:T(128)S(1)}, f32[32]{0:T(128)S(1)}) all-reduce(f32[32]{0:T(128)S(1)} %get-tuple-element.43, f32[32]{0:T(128)S(1)} %get-tuple-element.60), channel_id=1, replica_groups=mesh['row'=8,'col'=4] {'row','col'}, use_global_device_ids=true, to_apply=%region_10.11 | all-reduce | flops 64 | bytes 512 | tf_op jit(solution)/shard_map/psum | solution.py:110
  511.5 2.4 multiply_reduce_fusion.1
  514.2 1.0 copy-done.4
  515.2 4.2 collective-permute-start.10
  519.4 1.5 collective-permute-start.11
  520.9 4.1 collective-permute-done.11
  525.2 2.7 fusion.118
  527.9 3.2 copy.53
  531.2 1.3 collective-permute-start.12
  532.5 3.2 copy.55
  535.7 3.0 collective-permute-start.13
  538.7 3.6 copy.54
  542.3 3.6 copy.56
  545.9 4.6 fusion.51
  550.5 16.5 %fusion.92 = f32[32,256]{1,0:T(8,128)S(1)} fusion(f32[32,128,128]{2,0,1:T(8,128)S(1)} %fusion.51, f32[128,128]{1,0:T(8,128)S(1)} %copy-done.12, s32[128,128]{1,0:T(8,128)S(1)} %copy-done.13), kind=kOutput, calls=%fused_computation.116 | convolution fusion | flops 1619001344 | bytes 2260992 | tf_op jit(solution)/shard_map/dot_general | solution.py:92
  567.0 40.7 %all-reduce.1 = (f32[32,256]{1,0:T(8,128)S(1)}, f32[32]{0:T(128)S(1)}) all-reduce(f32[32,256]{1,0:T(8,128)S(1)} %fusion.92, f32[32]{0:T(128)S(1)} %get-tuple-element.32), channel_id=1, replica_groups=mesh['row'=8,'col'=4] {'row','col'}, use_global_device_ids=true, to_apply=%region_16.17 | all-reduce | flops 8224 | bytes 65792 | tf_op jit(solution)/shard_map/psum | solution.py:111
  608.0 17.9 %multiply_add_fusion.1 = f32[32,128,128]{2,0,1:T(8,128)S(1)} fusion(f32[32,128,128]{2,0,1:T(8,128)S(1)} %copy-done.3, f32[32,128,128]{2,0,1:T(8,128)} %copy-done.9, f32[32,256,1]{1,0,2:T(8,128)S(1)} %convolution_bitcast_fusion, f32[256,128,128]{0,2,1:T(8,128)} %copy-done, f32[32]{0:T(128)S(1)} %div.37), kind=kOutput, calls=%fused_computation.100 | convolution fusion | flops 1612185600 | bytes 23101568 | tf_op jit(solution)/shard_map/dot_general | solution.py:102
  625.9 18.9 %multiply_reduce_fusion = (f32[32]{0:T(128)S(1)}, f32[32,128,128]{2,0,1:T(8,128)}) fusion(f32[32,128,128]{2,0,1:T(8,128)S(1)} %multiply_add_fusion.1, f32[32,128,128]{2,0,1:T(8,128)S(1)} %copy-done.16, f32[32]{0:T(128)S(1)} %div.37, f32[32,256,1]{1,0,2:T(8,128)S(1)} %convolution_bitcast_fusion, f32[128,128]{1,0:T(8,128)S(1)} %copy-done.12, ...), kind=kOutput, calls=%fused_computation.99 | convolution fusion | flops 1622147072 | bytes 8618240 | tf_op jit(solution)/shard_map/dot_general | solution.py:97
  644.8 39.4 %psum.63 = f32[32]{0:T(128)S(1)} all-reduce(f32[32]{0:T(128)S(1)} %get-tuple-element.62), channel_id=1, replica_groups=mesh['row'=8,'col'=4] {'row','col'}, use_global_device_ids=true, to_apply=%region_18.19 | all-reduce | flops 32 | bytes 256 | tf_op jit(solution)/shard_map/psum | solution.py:125
  684.2 2.1 multiply_subtract_fusion
  686.4 2.5 copy.59
  688.9 17.3 %multiply_add_fusion = f32[32,128,128]{2,0,1:T(8,128)S(1)} fusion(f32[32,128,128]{2,0,1:T(8,128)S(1)} %copy-done.18, f32[32,128,128]{2,0,1:T(8,128)S(1)} %copy-done.17, f32[32,256,1]{1,0,2:T(8,128)S(1)} %convolution_bitcast_fusion.2, f32[128,128]{1,0:T(8,128)S(1)} %copy-done.12, s32[128,128]{1,0:T(8,128)S(1)} %copy-done.13, f32[32]{0:T(128)S(1)} %div.38, ...), kind=kOutput, calls=%fused_computation.98 | convolution fusion | flops 1621098496 | bytes 6455552 | tf_op jit(solution)/shard_map/dot_general | solution.py:97
  706.2 2.5 copy.58
  (91 shorter events, 6.6 us)
Async XLA Ops:
  7.2 250.8 %all-reduce.5.cloned.1.call-start = ((), (), s32[]{:S(2)}) async-start(), calls=%async_computation | async-start | bytes 524288 | tf_op jit(solution)/shard_map/psum | solution.py:89
  8.4 40.8 %collective-permute-start = (f32[128,1]{1,0:T(8,128)S(1)}, f32[128,1]{1,0:T(8,128)S(1)}, u32[]{:S(2)}, u32[]{:S(2)}) collective-permute-start(f32[128,1]{1,0:T(8,128)S(1)} %slice.188), channel_id=1, source_target_pairs={{0,1},{1,2},{2,3},{4,5},{5,6},{6,7},{8,9},{9,10},{10,11},{12,13},{... | collective-permute-start | bytes 1544 | tf_op jit(solution)/shard_map/ppermute | solution.py:14
  10.9 14.8 %copy-start.11 = (f32[32,128,128]{2,1,0:T(8,128)S(1)}, f32[32,128,128]{2,1,0:T(8,128)}, u32[]{:S(2)}) copy-start(f32[32,128,128]{2,1,0:T(8,128)} %param.8) | copy-start | bytes 6291460
  10.9 14.8 %copy-start.12 = (f32[128,128]{1,0:T(8,128)S(1)}, f32[128,128]{1,0:T(8,128)}, u32[]{:S(2)}) copy-start(f32[128,128]{1,0:T(8,128)} %param.10) | copy-start | bytes 196612
  10.9 14.8 %copy-start.13 = (s32[128,128]{1,0:T(8,128)S(1)}, s32[128,128]{1,0:T(8,128)}, u32[]{:S(2)}) copy-start(s32[128,128]{1,0:T(8,128)} %param.9) | copy-start | bytes 196612
  11.0 38.2 %collective-permute-start.1 = (f32[1,128]{1,0:T(1,128)S(1)}, f32[1,128]{1,0:T(1,128)S(1)}, u32[]{:S(2)}, u32[]{:S(2)}) collective-permute-start(f32[1,128]{1,0:T(1,128)S(1)} %slice.190), channel_id=1, source_target_pairs={{0,4},{4,8},{8,12},{12,16},{16,20},{20,24},{24,28},{1,5},{5,9},{9,... | collective-permute-start | bytes 1544 | tf_op jit(solution)/shard_map/ppermute | solution.py:14
  20.7 23.2 %copy-start.1 = (f32[256,128,128]{0,2,1:T(8,128)}, f32[256,128,128]{0,2,1:T(8,128)S(1)}, u32[]{:S(2)}) copy-start(f32[256,128,128]{0,2,1:T(8,128)S(1)} %fusion.28) | copy-start | bytes 50331652
  20.8 23.1 %collective-permute-start.2 = (f32[256,1,128]{0,2,1:T(8,128)S(1)}, f32[256,1,128]{0,2,1:T(8,128)S(1)}, u32[]{:S(2)}, u32[]{:S(2)}) collective-permute-start(f32[256,1,128]{0,2,1:T(8,128)S(1)} %get-tuple-element.42), channel_id=1, source_target_pairs={{0,4},{4,8},{8,12},{12,16},{16,20},{20,24},{24,28},{1,5},{5,9},{9,... | collective-permute-start | bytes 393224 | tf_op jit(solution)/shard_map/ppermute | solution.py:24
  24.2 19.5 %copy-start.14 = (s32[128,128]{1,0:T(8,128)S(1)}, s32[128,128]{1,0:T(8,128)}, u32[]{:S(2)}) copy-start(s32[128,128]{1,0:T(8,128)} %param.13) | copy-start | bytes 196612
  24.2 19.5 %copy-start.15 = (f32[8]{0:T(128)S(1)}, f32[8]{0:T(128)}, u32[]{:S(2)}) copy-start(f32[8]{0:T(128)} %param.15) | copy-start | bytes 100
  24.3 19.7 %collective-permute-start.3 = (f32[256,1,128]{0,2,1:T(8,128)S(1)}, f32[256,1,128]{0,2,1:T(8,128)S(1)}, u32[]{:S(2)}, u32[]{:S(2)}) collective-permute-start(f32[256,1,128]{0,2,1:T(8,128)S(1)} %get-tuple-element.41), channel_id=1, source_target_pairs={{4,0},{8,4},{12,8},{16,12},{20,16},{24,20},{28,24},{5,1},{9,5},{13... | collective-permute-start | bytes 393224 | tf_op jit(solution)/shard_map/ppermute | solution.py:25
  44.1 5.2 collective-permute-start.4
  45.4 4.7 collective-permute-start.5
  81.5 5.7 copy-start
  340.7 4.8 collective-permute-start.6
  344.1 5.6 collective-permute-start.7
  355.9 7.7 %collective-permute-start.8 = (f32[32,130,1]{1,0,2:T(8,128)S(1)}, f32[32,130,1]{1,0,2:T(8,128)S(1)}, u32[]{:S(2)}, u32[]{:S(2)}) collective-permute-start(f32[32,130,1]{1,0,2:T(8,128)S(1)} %copy.48), channel_id=1, source_target_pairs={{1,0},{2,1},{3,2},{5,4},{6,5},{7,6},{9,8},{10,9},{11,10},{13,12},{... | collective-permute-start | bytes 49928 | tf_op jit(solution)/shard_map/ppermute | solution.py:25
  360.4 6.8 collective-permute-start.9
  375.4 1.3 copy-start.10
  433.7 17.9 %copy-start.8 = (f32[32,128,128]{2,0,1:T(8,128)S(1)}, f32[32,128,128]{2,0,1:T(8,128)}, u32[]{:S(2)}) copy-start(f32[32,128,128]{2,0,1:T(8,128)} %get-tuple-element.59) | copy-start | bytes 6291460
  451.5 59.9 %copy-start.2 = (f32[32,128,128]{2,0,1:T(8,128)}, f32[32,128,128]{2,0,1:T(8,128)S(1)}, u32[]{:S(2)}) copy-start(f32[32,128,128]{2,0,1:T(8,128)S(1)} %fusion.76) | copy-start | bytes 6291460
  513.9 1.4 copy-start.4
  515.2 5.7 collective-permute-start.10
  519.4 5.6 collective-permute-start.11
  531.2 7.6 %collective-permute-start.12 = (f32[32,130,1]{1,0,2:T(8,128)S(1)}, f32[32,130,1]{1,0,2:T(8,128)S(1)}, u32[]{:S(2)}, u32[]{:S(2)}) collective-permute-start(f32[32,130,1]{1,0,2:T(8,128)S(1)} %copy.53), channel_id=1, source_target_pairs={{1,0},{2,1},{3,2},{5,4},{6,5},{7,6},{9,8},{10,9},{11,10},{13,12},{... | collective-permute-start | bytes 49928 | tf_op jit(solution)/shard_map/ppermute | solution.py:25
  535.7 6.6 collective-permute-start.13
  550.5 16.5 %copy-start.9 = (f32[32,128,128]{2,0,1:T(8,128)}, f32[32,128,128]{2,0,1:T(8,128)S(1)}, u32[]{:S(2)}) copy-start(f32[32,128,128]{2,0,1:T(8,128)S(1)} %fusion.51) | copy-start | bytes 6291460
  550.5 57.5 %copy-start.3 = (f32[32,128,128]{2,0,1:T(8,128)S(1)}, f32[32,128,128]{2,0,1:T(8,128)}, u32[]{:S(2)}) copy-start(f32[32,128,128]{2,0,1:T(8,128)} %copy-done.2) | copy-start | bytes 6291460
  608.0 17.9 %copy-start.5 = (f32[32,128,128]{2,0,1:T(8,128)S(1)}, f32[32,128,128]{2,0,1:T(8,128)}, u32[]{:S(2)}) copy-start(f32[32,128,128]{2,0,1:T(8,128)} %copy-done.4) | copy-start | bytes 6291460
  608.0 17.9 %copy-start.16 = (f32[32,128,128]{2,0,1:T(8,128)S(1)}, f32[32,128,128]{2,0,1:T(8,128)}, u32[]{:S(2)}) copy-start(f32[32,128,128]{2,0,1:T(8,128)} %get-tuple-element.61) | copy-start | bytes 6291460
  625.9 18.9 %copy-start.7 = (f32[32,128,128]{2,0,1:T(8,128)}, f32[32,128,128]{2,0,1:T(8,128)S(1)}, u32[]{:S(2)}) copy-start(f32[32,128,128]{2,0,1:T(8,128)S(1)} %multiply_add_fusion.1) | copy-start | bytes 6291460
  625.9 58.3 %copy-start.6 = (f32[32,128,128]{2,0,1:T(8,128)S(1)}, f32[32,128,128]{2,0,1:T(8,128)}, u32[]{:S(2)}) copy-start(f32[32,128,128]{2,0,1:T(8,128)} %copy-done.4) | copy-start | bytes 6291460
  686.4 2.6 copy-start.17
  686.4 2.6 copy-start.18
Sparse Core Ops, SparseCore 0:
  125.8 132.1 all-reduce.4
where the time goes:
time: 722 us; the launch traced here: 716 us
  blocking collectives  205 us (28%)
  matrix products  203 us (28%)
  other arithmetic  108 us (15%)
  waiting for transfers between devices  96.4 us (13%)
  local copies, waits for them, and re-layouts  51.1 us (7%)
  starting transfers between devices  35.9 us (5%)
  between operations  16.7 us (2%)
    psum x1, waiting for transfers between devices, body(): inverse = invert(lax.psum(partial_matrix, ('row', 'col')))  87.1 us
    psum x2, blocking collectives, refresh(): projected = lax.psum(project(field_image), ('row', 'col'))  81 us
    dot_general x3, matrix products, expand(): jnp.dot(coarse, basis_flat, precision=precise)  56.2 us
    dot_general x3, matrix products, correction_image(): jnp.dot(coarse, image_flat, precision=precise)  54.2 us
    dot_general x3, matrix products, project(): lax.dot_general(field.reshape(load_count, tile_cells), basis_flat, contra...  51 us
    psum x1, blocking collectives, body(): load_sums = lax.psum(project(load_currents), ('row', 'col'))  45.2 us
    sub x3, other arithmetic, stencil(): diagonal * centre - right_link * padded[:, 1:-1, 2:]  40.6 us
    psum x1, blocking collectives, refresh(): weighted_norm = lax.psum(local_norm, ('row', 'col'))  39.8 us
  transfers between devices with their start and end apart: 15, of which 5 were waited for; matrix products, arithmetic and copies ran while one was open for 5% of the time, Pallas kernels for 0%

commit v1 on v0

--- a/solution.py
+++ b/solution.py
@@ -108,7 +108,7 @@
         local_norm = jnp.sum(residual * scaled, axis=(1, 2))
         field_image = stencil(extended(scaled, (("row", 1), ("col", 2)), 1), coeffs)
         weighted_norm = lax.psum(local_norm, ("row", "col"))
-        projected = lax.psum(project(field_image), ("row", "col"))
+        projected = jnp.sum(lax.all_gather(project(field_image), ("row", "col")), axis=0)
         coarse = jnp.dot(projected, inverse, precision=precise)
         return (scaled, weighted_norm, field_image, coarse)
 

time: 722 us -> 752 us (1.042)
  waiting for transfers between devices: 96.4 us -> 163 us
  blocking collectives: 205 us -> 164 us
    psum x2 -> x0, blocking collectives: 81 us -> none  [refresh(): projected = lax.psum(project(field_image), ('row', 'col'))]
    all_gather x0 -> x2, waiting for transfers between devices: none -> 66.5 us  [refresh(): lax.all_gather(project(field_image), ('row', 'col'))]
    psum x1 -> x2, blocking collectives: 39.8 us -> 79.5 us  [refresh(): weighted_norm = lax.psum(local_norm, ('row', 'col'))]
  transfers between devices with their start and end apart: 15 -> 17, of which waited for: 5 -> 7; matrix products, arithmetic and copies ran while one was open for 5% -> 5% of each run, Pallas kernels for 0% -> 0%
where the time goes in v1:
time: 752 us; the launch traced here: 746 us
  matrix products  204 us (27%)
  blocking collectives  164 us (22%)
  waiting for transfers between devices  163 us (22%)
  other arithmetic  111 us (15%)
  local copies, waits for them, and re-layouts  52.4 us (7%)
  starting transfers between devices  35.9 us (5%)
  between operations  16.3 us (2%)
    psum x1, waiting for transfers between devices, body(): inverse = invert(lax.psum(partial_matrix, ('row', 'col')))  87.1 us
    psum x2, blocking collectives, refresh(): weighted_norm = lax.psum(local_norm, ('row', 'col'))  79.5 us
    all_gather x2, waiting for transfers between devices, refresh(): lax.all_gather(project(field_image), ('row', 'col'))  66.5 us
    dot_general x3, matrix products, expand(): jnp.dot(coarse, basis_flat, precision=precise)  56.2 us
    dot_general x3, matrix products, correction_image(): jnp.dot(coarse, image_flat, precision=precise)  54.2 us
    dot_general x3, matrix products, project(): lax.dot_general(field.reshape(load_count, tile_cells), basis_flat, contra...  52.1 us
    psum x1, blocking collectives, body(): load_sums = lax.psum(project(load_currents), ('row', 'col'))  45.2 us
    sub x3, other arithmetic, stencil(): diagonal * centre - right_link * padded[:, 1:-1, 2:]  40.6 us
  transfers between devices with their start and end apart: 17, of which 7 were waited for; matrix products, arithmetic and copies ran while one was open for 5% of the time, Pallas kernels for 0%

profile of v1, /device:TPU:0, one launch (start us, length us, event | category | flops | bytes accessed | tf_op | source)
XLA Modules:
  0.0 746.2 jit_solution(12452373309344205350)
XLA Ops:
  8.4 2.4 collective-permute-start
  11.0 4.4 collective-permute-start.1
  15.3 5.4 fusion.28
  20.8 3.4 collective-permute-start.2
  24.3 1.4 collective-permute-start.3
  25.7 18.0 %fusion.84 = f32[32,256]{1,0:T(8,128)S(1)} fusion(f32[32,128,128]{2,1,0:T(8,128)S(1)} %copy-done.11, f32[128,128]{1,0:T(8,128)S(1)} %copy-done.12, s32[128,128]{1,0:T(8,128)S(1)} %copy-done.13), kind=kOutput, calls=%fused_computation.114 | convolution fusion | flops 1619001344 | bytes 2260992 | tf_op jit(solution)/shard_map/dot_general | solution.py:92
  44.1 1.3 collective-permute-start.4
  45.4 3.8 collective-permute-start.5
  50.1 31.3 %fusion.17 = f32[256,128,128]{0,2,1:T(8,128)S(1)} fusion(f32[256,128,128]{0,2,1:T(8,128)} %copy-done.1, f32[256,1,128]{0,2,1:T(8,128)S(1)} %collective-permute-done.2, f32[256,1,128]{0,2,1:T(8,128)S(1)} %collective-permute-done.3, f32[256,130,1]{0,2,1:T(1,128)S(1)} %collective-permute-done.5, f32[256,130,1]{0,2,1:T(1,128)S(1)} %collective-permute-done.4, ...), kind=kLoop, calls=%fused_computation.20 | loop fusion | flops 79691776 | bytes 34541568 | tf_op jit(solution)/shard_map/sub | solution.py:39
  81.5 5.7 copy-done
  87.2 38.4 %fusion.81 = f32[256,256]{0,1:T(8,128)} fusion(f32[256,128,128]{0,2,1:T(8,128)S(1)} %fusion.17, f32[128,128]{1,0:T(8,128)S(1)} %copy-done.12, s32[128,128]{1,0:T(8,128)S(1)} %copy-done.13), kind=kOutput, calls=%fused_computation.110 | convolution fusion | flops 12893290496 | bytes 17170432 | tf_op jit(solution)/shard_map/dot_general | solution.py:88
  125.7 45.2 %psum.42 = f32[32,256]{1,0:T(8,128)S(1)} all-reduce(f32[32,256]{1,0:T(8,128)S(1)} %fusion.84), channel_id=1, replica_groups=mesh['row'=8,'col'=4] {'row','col'}, use_global_device_ids=true, to_apply=%region_0.1 | all-reduce | flops 8192 | bytes 65536 | tf_op jit(solution)/shard_map/psum | solution.py:115
  171.0 87.1 %all-reduce.4.cloned.1.call-done = f32[256,256]{0,1:T(8,128)} async-done(((f32[256,256]{0,1:T(8,128)}), f32[256,256]{0,1:T(8,128)}) %all-reduce.4.cloned.1.call-update) | async-done | bytes 262160 | tf_op jit(solution)/shard_map/psum | solution.py:89
  258.1 1.1 copy.48
  260.1 11.7 %cholesky.53 = f32[128,128]{1,0:T(8,128)S(1)} custom-call(f32[128,128]{1,0:T(8,128)S(1)} %cholesky.121), custom_call_target="Cholesky" | custom-call | tf_op jit(solution)/shard_map/jit(cholesky)/cholesky | solution.py:48
  271.9 9.8 %custom-call.16 = f32[1,128,128]{1,2,0:T(8,128)S(1)} custom-call(f32[1,128,128]{2,1,0:T(8,128)S(1)} %get-tuple-element.54), custom_call_target="InvertDiagBlocksLowerTriangular" | custom-call | tf_op jit(solution)/shard_map/jit(cholesky)/cholesky | solution.py:48
  282.2 11.7 %cholesky.108 = f32[128,128]{1,0:T(8,128)S(1)} custom-call(f32[128,128]{1,0:T(8,128)S(1)} %convolution_subtract_fusion.2), custom_call_target="Cholesky" | custom-call | tf_op jit(solution)/shard_map/jit(cholesky)/cholesky | solution.py:48
  296.1 4.1 while.1
  296.7 1.4 bitcast_dynamic-update-slice_fusion.2
  298.8 1.4 bitcast_dynamic-update-slice_fusion.2
  300.2 20.1 %custom-call.17 = f32[2,128,128]{1,2,0:T(8,128)S(1)} custom-call(f32[2,128,128]{2,1,0:T(8,128)S(1)} %get-tuple-element.9), custom_call_target="InvertDiagBlocksLowerTriangular" | custom-call | tf_op jit(solution)/shard_map/triangular_solve | solution.py:51
  322.3 18.5 %multiply_reduce_fusion.3 = (f32[32]{0:T(128)S(1)}, f32[32,128,128]{2,0,1:T(8,128)S(1)}, f32[32,128,128]{2,0,1:T(8,128)}) fusion(f32[128,128]{1,0:T(8,128)S(1)} %get-tuple-element.32, f32[32,256,1]{1,0,2:T(8,128)S(1)} %convolution_bitcast_fusion.2, f32[256,128,128]{0,2,1:T(8,128)} %copy-done, f32[32,128,128]{2,1,0:T(8,128)} %param.8), kind=kOutput, calls=%fused_computation.105 | convolution fusion | flops 1612709888 | bytes 23167104 | tf_op jit(solution)/shard_map/dot_general | solution.py:102
  340.8 3.4 collective-permute-start.6
  344.2 1.3 collective-permute-start.7
  345.6 4.2 collective-permute-done.7
  350.0 2.7 fusion.119
  352.7 3.2 copy.50
  355.9 1.3 collective-permute-start.8
  357.2 3.2 copy.52
  360.4 3.2 collective-permute-start.9
  363.6 3.6 copy.51
  367.2 3.6 copy.53
  370.8 4.6 fusion.59
  375.4 1.3 copy-done.10
  376.7 17.0 %fusion.89 = f32[32,256]{1,0:T(8,128)} fusion(f32[32,128,128]{2,0,1:T(8,128)S(1)} %fusion.59, f32[128,128]{1,0:T(8,128)S(1)} %copy-done.12, s32[128,128]{1,0:T(8,128)S(1)} %copy-done.13), kind=kOutput, calls=%fused_computation.115 | convolution fusion | flops 1619001344 | bytes 2260992 | tf_op jit(solution)/shard_map/dot_general | solution.py:92
  393.8 53.6 %all-gather.5.cloned.1.call-done = f32[1024,256]{1,0:T(8,128)} async-done(((f32[32,256]{1,0:T(8,128)}), f32[1024,256]{1,0:T(8,128)}) %all-gather.5.cloned.1.call-update) | async-done | bytes 1048592 | tf_op jit(solution)/shard_map/all_gather | solution.py:111
  447.4 1.3 reduce_sum.85
  449.0 17.8 %fusion.76 = f32[32,128,128]{2,0,1:T(8,128)S(1)} fusion(f32[32,128,128]{2,0,1:T(8,128)} %copy-done.10, f32[32,256,1]{1,0,2:T(8,128)S(1)} %convolution_bitcast_fusion.1, f32[256,128,128]{0,2,1:T(8,128)} %copy-done), kind=kOutput, calls=%fused_computation.109 | convolution fusion | flops 1611137024 | bytes 21004288 | tf_op jit(solution)/shard_map/dot_general | solution.py:102
  466.9 20.1 %multiply_reduce_fusion.2 = (f32[32]{0:T(128)S(1)}, f32[32,128,128]{2,0,1:T(8,128)}) fusion(f32[32,128,128]{2,0,1:T(8,128)S(1)} %fusion.76, f32[32,256,1]{1,0,2:T(8,128)S(1)} %convolution_bitcast_fusion.1, f32[128,128]{1,0:T(8,128)S(1)} %copy-done.12, s32[128,128]{1,0:T(8,128)S(1)} %copy-done.13, f32[32,128,128]{2,0,1:T(8,128)S(1)} %copy-done.8, ...), kind=kOutput, calls=%fused_computation.104 | convolution fusion | flops 1621098496 | bytes 6520960 | tf_op jit(solution)/shard_map/dot_general | solution.py:97
  486.9 39.3 %all-reduce.1 = (f32[32]{0:T(128)S(1)}, f32[32]{0:T(128)S(1)}) all-reduce(f32[32]{0:T(128)S(1)} %get-tuple-element.41, f32[32]{0:T(128)S(1)} %get-tuple-element.58), channel_id=1, replica_groups=mesh['row'=8,'col'=4] {'row','col'}, use_global_device_ids=true, to_apply=%region_10.11 | all-reduce | flops 64 | bytes 512 | tf_op jit(solution)/shard_map/psum | solution.py:110
  526.2 2.4 multiply_reduce_fusion.1
  530.0 4.2 collective-permute-start.10
  534.2 1.5 collective-permute-start.11
  535.7 4.1 collective-permute-done.11
  540.0 2.7 fusion.118
  542.7 3.2 copy.55
  545.9 1.3 collective-permute-start.12
  547.2 3.2 copy.57
  550.4 3.0 collective-permute-start.13
  553.5 3.6 copy.56
  557.0 3.6 copy.58
  560.6 4.6 fusion.51
  565.3 1.3 copy-done.9
  566.6 17.0 %fusion.92 = f32[32,256]{1,0:T(8,128)} fusion(f32[32,128,128]{2,0,1:T(8,128)S(1)} %fusion.51, f32[128,128]{1,0:T(8,128)S(1)} %copy-done.12, s32[128,128]{1,0:T(8,128)S(1)} %copy-done.13), kind=kOutput, calls=%fused_computation.116 | convolution fusion | flops 1619001344 | bytes 2260992 | tf_op jit(solution)/shard_map/dot_general | solution.py:92
  583.6 40.2 %psum.46 = f32[32]{0:T(128)S(1)} all-reduce(f32[32]{0:T(128)S(1)} %get-tuple-element.30), channel_id=1, replica_groups=mesh['row'=8,'col'=4] {'row','col'}, use_global_device_ids=true, to_apply=%region_15.16 | all-reduce | flops 32 | bytes 256 | tf_op jit(solution)/shard_map/psum | solution.py:110
  623.8 12.8 %all-gather.7.cloned.1.call-done = f32[1024,256]{1,0:T(8,128)} async-done(((f32[32,256]{1,0:T(8,128)}), f32[1024,256]{1,0:T(8,128)}) %all-gather.7.cloned.1.call-update) | async-done | bytes 1048592 | tf_op jit(solution)/shard_map/all_gather | solution.py:111
  636.6 1.3 reduce_sum.88
  638.2 17.9 %multiply_add_fusion.1 = f32[32,128,128]{2,0,1:T(8,128)S(1)} fusion(f32[32,128,128]{2,0,1:T(8,128)S(1)} %copy-done.3, f32[32,128,128]{2,0,1:T(8,128)} %copy-done.9, f32[32,256,1]{1,0,2:T(8,128)S(1)} %convolution_bitcast_fusion, f32[256,128,128]{0,2,1:T(8,128)} %copy-done, f32[32]{0:T(128)S(1)} %div.37), kind=kOutput, calls=%fused_computation.100 | convolution fusion | flops 1612185600 | bytes 23101568 | tf_op jit(solution)/shard_map/dot_general | solution.py:102
  656.1 18.9 %multiply_reduce_fusion = (f32[32]{0:T(128)S(1)}, f32[32,128,128]{2,0,1:T(8,128)}) fusion(f32[32,128,128]{2,0,1:T(8,128)S(1)} %multiply_add_fusion.1, f32[32,128,128]{2,0,1:T(8,128)S(1)} %copy-done.16, f32[32]{0:T(128)S(1)} %div.37, f32[32,256,1]{1,0,2:T(8,128)S(1)} %convolution_bitcast_fusion, f32[128,128]{1,0:T(8,128)S(1)} %copy-done.12, ...), kind=kOutput, calls=%fused_computation.99 | convolution fusion | flops 1622147072 | bytes 8618240 | tf_op jit(solution)/shard_map/dot_general | solution.py:97
  675.0 39.7 %psum.47 = f32[32]{0:T(128)S(1)} all-reduce(f32[32]{0:T(128)S(1)} %get-tuple-element.60), channel_id=1, replica_groups=mesh['row'=8,'col'=4] {'row','col'}, use_global_device_ids=true, to_apply=%region_18.19 | all-reduce | flops 32 | bytes 256 | tf_op jit(solution)/shard_map/psum | solution.py:125
  714.7 2.1 multiply_subtract_fusion
  716.8 2.5 copy.61
  719.4 17.3 %multiply_add_fusion = f32[32,128,128]{2,0,1:T(8,128)S(1)} fusion(f32[32,128,128]{2,0,1:T(8,128)S(1)} %copy-done.18, f32[32,128,128]{2,0,1:T(8,128)S(1)} %copy-done.17, f32[32,256,1]{1,0,2:T(8,128)S(1)} %convolution_bitcast_fusion.2, f32[128,128]{1,0:T(8,128)S(1)} %copy-done.12, s32[128,128]{1,0:T(8,128)S(1)} %copy-done.13, f32[32]{0:T(128)S(1)} %div.38, ...), kind=kOutput, calls=%fused_computation.98 | convolution fusion | flops 1621098496 | bytes 6455552 | tf_op jit(solution)/shard_map/dot_general | solution.py:97
  736.6 2.5 copy.60
  (98 shorter events, 10.6 us)
Async XLA Ops:
  7.2 250.9 %all-reduce.4.cloned.1.call-start = ((), (), s32[]{:S(2)}) async-start(), calls=%async_computation | async-start | bytes 524288 | tf_op jit(solution)/shard_map/psum | solution.py:89
  8.4 40.8 %collective-permute-start = (f32[128,1]{1,0:T(8,128)S(1)}, f32[128,1]{1,0:T(8,128)S(1)}, u32[]{:S(2)}, u32[]{:S(2)}) collective-permute-start(f32[128,1]{1,0:T(8,128)S(1)} %slice.188), channel_id=1, source_target_pairs={{0,1},{1,2},{2,3},{4,5},{5,6},{6,7},{8,9},{9,10},{10,11},{12,13},{... | collective-permute-start | bytes 1544 | tf_op jit(solution)/shard_map/ppermute | solution.py:14
  10.9 14.8 %copy-start.11 = (f32[32,128,128]{2,1,0:T(8,128)S(1)}, f32[32,128,128]{2,1,0:T(8,128)}, u32[]{:S(2)}) copy-start(f32[32,128,128]{2,1,0:T(8,128)} %param.8) | copy-start | bytes 6291460
  10.9 14.8 %copy-start.12 = (f32[128,128]{1,0:T(8,128)S(1)}, f32[128,128]{1,0:T(8,128)}, u32[]{:S(2)}) copy-start(f32[128,128]{1,0:T(8,128)} %param.10) | copy-start | bytes 196612
  10.9 14.8 %copy-start.13 = (s32[128,128]{1,0:T(8,128)S(1)}, s32[128,128]{1,0:T(8,128)}, u32[]{:S(2)}) copy-start(s32[128,128]{1,0:T(8,128)} %param.9) | copy-start | bytes 196612
  11.0 38.2 %collective-permute-start.1 = (f32[1,128]{1,0:T(1,128)S(1)}, f32[1,128]{1,0:T(1,128)S(1)}, u32[]{:S(2)}, u32[]{:S(2)}) collective-permute-start(f32[1,128]{1,0:T(1,128)S(1)} %slice.190), channel_id=1, source_target_pairs={{0,4},{4,8},{8,12},{12,16},{16,20},{20,24},{24,28},{1,5},{5,9},{9,... | collective-permute-start | bytes 1544 | tf_op jit(solution)/shard_map/ppermute | solution.py:14
  20.7 23.2 %copy-start.1 = (f32[256,128,128]{0,2,1:T(8,128)}, f32[256,128,128]{0,2,1:T(8,128)S(1)}, u32[]{:S(2)}) copy-start(f32[256,128,128]{0,2,1:T(8,128)S(1)} %fusion.28) | copy-start | bytes 50331652
  20.8 23.1 %collective-permute-start.2 = (f32[256,1,128]{0,2,1:T(8,128)S(1)}, f32[256,1,128]{0,2,1:T(8,128)S(1)}, u32[]{:S(2)}, u32[]{:S(2)}) collective-permute-start(f32[256,1,128]{0,2,1:T(8,128)S(1)} %get-tuple-element.40), channel_id=1, source_target_pairs={{0,4},{4,8},{8,12},{12,16},{16,20},{20,24},{24,28},{1,5},{5,9},{9,... | collective-permute-start | bytes 393224 | tf_op jit(solution)/shard_map/ppermute | solution.py:24
  24.2 19.5 %copy-start.14 = (s32[128,128]{1,0:T(8,128)S(1)}, s32[128,128]{1,0:T(8,128)}, u32[]{:S(2)}) copy-start(s32[128,128]{1,0:T(8,128)} %param.13) | copy-start | bytes 196612
  24.2 19.5 %copy-start.15 = (f32[8]{0:T(128)S(1)}, f32[8]{0:T(128)}, u32[]{:S(2)}) copy-start(f32[8]{0:T(128)} %param.15) | copy-start | bytes 100
  24.3 19.7 %collective-permute-start.3 = (f32[256,1,128]{0,2,1:T(8,128)S(1)}, f32[256,1,128]{0,2,1:T(8,128)S(1)}, u32[]{:S(2)}, u32[]{:S(2)}) collective-permute-start(f32[256,1,128]{0,2,1:T(8,128)S(1)} %get-tuple-element.39), channel_id=1, source_target_pairs={{4,0},{8,4},{12,8},{16,12},{20,16},{24,20},{28,24},{5,1},{9,5},{13... | collective-permute-start | bytes 393224 | tf_op jit(solution)/shard_map/ppermute | solution.py:25
  44.1 5.2 collective-permute-start.4
  45.4 4.7 collective-permute-start.5
  81.5 5.7 copy-start
  125.7 321.8 %all-gather.5.cloned.1.call-start = ((), (), s32[]{:S(2)}) async-start(), calls=%async_computation.1 | async-start | bytes 1081344 | tf_op jit(solution)/shard_map/all_gather | solution.py:111
  340.8 4.8 collective-permute-start.6
  344.2 5.6 collective-permute-start.7
  355.9 7.7 %collective-permute-start.8 = (f32[32,130,1]{1,0,2:T(8,128)S(1)}, f32[32,130,1]{1,0,2:T(8,128)S(1)}, u32[]{:S(2)}, u32[]{:S(2)}) collective-permute-start(f32[32,130,1]{1,0,2:T(8,128)S(1)} %copy.50), channel_id=1, source_target_pairs={{1,0},{2,1},{3,2},{5,4},{6,5},{7,6},{9,8},{10,9},{11,10},{13,12},{... | collective-permute-start | bytes 49928 | tf_op jit(solution)/shard_map/ppermute | solution.py:25
  360.4 6.8 collective-permute-start.9
  375.4 1.3 copy-start.10
  393.8 242.9 %all-gather.7.cloned.1.call-start = ((), (), s32[]{:S(2)}) async-start(), calls=%async_computation.2 | async-start | bytes 1081344 | tf_op jit(solution)/shard_map/all_gather | solution.py:111
  449.0 17.9 %copy-start.8 = (f32[32,128,128]{2,0,1:T(8,128)S(1)}, f32[32,128,128]{2,0,1:T(8,128)}, u32[]{:S(2)}) copy-start(f32[32,128,128]{2,0,1:T(8,128)} %get-tuple-element.57) | copy-start | bytes 6291460
  466.8 59.4 %copy-start.2 = (f32[32,128,128]{2,0,1:T(8,128)}, f32[32,128,128]{2,0,1:T(8,128)S(1)}, u32[]{:S(2)}) copy-start(f32[32,128,128]{2,0,1:T(8,128)S(1)} %fusion.76) | copy-start | bytes 6291460
  528.6 1.4 copy-start.4
  530.0 5.7 collective-permute-start.10
  534.2 5.6 collective-permute-start.11
  545.9 7.6 %collective-permute-start.12 = (f32[32,130,1]{1,0,2:T(8,128)S(1)}, f32[32,130,1]{1,0,2:T(8,128)S(1)}, u32[]{:S(2)}, u32[]{:S(2)}) collective-permute-start(f32[32,130,1]{1,0,2:T(8,128)S(1)} %copy.55), channel_id=1, source_target_pairs={{1,0},{2,1},{3,2},{5,4},{6,5},{7,6},{9,8},{10,9},{11,10},{13,12},{... | collective-permute-start | bytes 49928 | tf_op jit(solution)/shard_map/ppermute | solution.py:25
  550.4 6.6 collective-permute-start.13
  565.3 1.3 copy-start.9
  566.6 71.6 %copy-start.3 = (f32[32,128,128]{2,0,1:T(8,128)S(1)}, f32[32,128,128]{2,0,1:T(8,128)}, u32[]{:S(2)}) copy-start(f32[32,128,128]{2,0,1:T(8,128)} %copy-done.2) | copy-start | bytes 6291460
  638.2 17.9 %copy-start.5 = (f32[32,128,128]{2,0,1:T(8,128)S(1)}, f32[32,128,128]{2,0,1:T(8,128)}, u32[]{:S(2)}) copy-start(f32[32,128,128]{2,0,1:T(8,128)} %copy-done.4) | copy-start | bytes 6291460
  638.2 17.9 %copy-start.16 = (f32[32,128,128]{2,0,1:T(8,128)S(1)}, f32[32,128,128]{2,0,1:T(8,128)}, u32[]{:S(2)}) copy-start(f32[32,128,128]{2,0,1:T(8,128)} %get-tuple-element.59) | copy-start | bytes 6291460
  656.1 18.9 %copy-start.7 = (f32[32,128,128]{2,0,1:T(8,128)}, f32[32,128,128]{2,0,1:T(8,128)S(1)}, u32[]{:S(2)}) copy-start(f32[32,128,128]{2,0,1:T(8,128)S(1)} %multiply_add_fusion.1) | copy-start | bytes 6291460
  656.1 58.6 %copy-start.6 = (f32[32,128,128]{2,0,1:T(8,128)S(1)}, f32[32,128,128]{2,0,1:T(8,128)}, u32[]{:S(2)}) copy-start(f32[32,128,128]{2,0,1:T(8,128)} %copy-done.4) | copy-start | bytes 6291460
  716.8 2.6 copy-start.17
  716.8 2.6 copy-start.18
Sparse Core Ops, SparseCore 0:
  125.8 132.2 all-reduce.3
  393.9 53.5 all-gather.4
  583.7 52.8 all-gather.6
